TPU v7x, 32 devices: a whole 2x2x4 slice. The times are simulated.
32 devices in a mesh: row: 8 (over z, core), col: 4 (over y, x).
Axes of the slice: x: 2, y: 2, z: 4, core: 2. Of those that a mesh axis runs over, the one named last changes fastest.
Arguments:
- kkt: float32 [16384, 8, 4, 512], P('row', None, 'col'), as said below
- flow_grad: float32 [16384, 256], P(('row', 'col')), may hold values from -18 to 18
- perm: int32 [16384], P(('row', 'col')), may hold values from 0 to 16383, as said below
Outputs:
- line_grad: float32 [16384, 256], P(('row', 'col'))
- true_residual: float32 [16384, 256], P(('row', 'col'))
Inputs may be any that keep to these rules, and one draw needn't show every extreme that they name: Read as a 16384 x 16384 matrix as in the first step, kkt is symmetric and positive definite. perm is a permutation. The 512 lines of each aligned block (lines f * 512 to (f + 1) * 512 - 1) have at most 32 of their KKT rows in any one aligned block of 512 KKT rows, and exactly 32 in some.
All inputs are finite; a program needn't handle non-finite values.
Results may differ from a plain program's by a relative error of at most 0.0003.
Values sent between devices are 32-bit elements; how exact they have to be, the bound alone decides.
No kernel may reach another device: no remote copies, remote signals or barrier semaphores. Data moves between devices by JAX's collectives and lax.ppermute only.
A program may use at most 256 MiB of HBM per device.

v0:
```python
import jax
import jax.numpy as jnp
from jax import lax
from jax.sharding import PartitionSpec as P

ITERS = 2


relaxation = 0.15


def gram_matrix(left, right):
    return lax.dot_general(
        left,
        right,
        (((0,), (0,)), ((), ())),
        precision=lax.Precision.HIGHEST,
        preferred_element_type=jnp.float32,
    )


def times_small(left, right):
    return jnp.dot(left, right, precision=lax.Precision.HIGHEST, preferred_element_type=jnp.float32)


def solve_definite(matrix, right):
    factor = jnp.linalg.cholesky(matrix)
    return jax.scipy.linalg.cho_solve((factor, True), right)


def residual_gram(residual):
    return lax.psum(gram_matrix(residual, residual), ("row", "col"))


def on_device(kkt, flow_grad, perm):
    highest = lax.Precision.HIGHEST
    device_count = lax.axis_size("row") * lax.axis_size("col")
    block_rows, interval_count = flow_grad.shape
    capacity = 2 * max(1, block_rows // device_count)
    slot_total = device_count * capacity
    kkt_tile = kkt.reshape(kkt.shape[0], kkt.shape[1] * kkt.shape[3])
    owner = perm // block_rows
    local_row = perm % block_rows
    position = jnp.arange(block_rows)
    earlier = (owner[None, :] == owner[:, None]) & (position[None, :] < position[:, None])
    slot_index = jnp.sum(earlier.astype(jnp.int32), axis=1)
    slot_key = owner * capacity + slot_index
    onehot = jnp.arange(slot_total)[:, None] == slot_key[None, :]
    selector = onehot.astype(jnp.float32)
    send_rows = jnp.dot(selector, flow_grad, precision=highest, preferred_element_type=jnp.float32)
    send_index = jnp.sum(jnp.where(onehot, local_row[None, :] + 1, 0), axis=1) - 1
    received, received_index = (
        lax.all_to_all(
            send_rows.reshape(device_count, capacity, interval_count),
            ("row", "col"),
            split_axis=0,
            concat_axis=0,
            tiled=True,
        ),
        lax.all_to_all(
            send_index.reshape(device_count, capacity),
            ("row", "col"),
            split_axis=0,
            concat_axis=0,
            tiled=True,
        ),
    )
    landing = (position[:, None] == received_index.reshape(slot_total)[None, :]).astype(jnp.float32)
    rhs = jnp.dot(
        landing,
        received.reshape(slot_total, interval_count),
        precision=highest,
        preferred_element_type=jnp.float32,
    )

    def apply_operator(vector):
        partial_rows = jnp.dot(
            kkt_tile,
            lax.all_gather(vector, "row", axis=0, tiled=True),
            precision=highest,
            preferred_element_type=jnp.float32,
        )
        return lax.psum_scatter(partial_rows, "col", scatter_dimension=0, tiled=True)

    solution = jnp.zeros_like(rhs)
    residual = rhs
    direction = rhs
    norm_gram = residual_gram(residual)
    for iteration in range(ITERS):
        applied = apply_operator(direction)
        finished = iteration + 1 == ITERS
        curvature = lax.psum(gram_matrix(direction, applied), ("row", "col"))
        step_coef = solve_definite(curvature, norm_gram)
        solution = solution + times_small(direction, step_coef)
        residual = residual - times_small(applied, step_coef)
        if not finished:
            fresh = residual_gram(residual)
        if not finished:
            mixing = solve_definite(norm_gram, fresh)
            direction = residual + times_small(direction, mixing)
            norm_gram = fresh
    refined = solution + relaxation * residual
    true_residual = rhs - apply_operator(refined)
    back_rows = gram_matrix(landing, refined)
    returned = lax.all_to_all(
        back_rows.reshape(device_count, capacity, interval_count),
        ("row", "col"),
        split_axis=0,
        concat_axis=0,
        tiled=True,
    )
    line_grad = -gram_matrix(selector, returned.reshape(slot_total, interval_count))
    return (line_grad, true_residual)


def solution(mesh):
    in_specs = (P("row", None, "col", None), P(("row", "col"), None), P(("row", "col")))
    out_specs = (P(("row", "col"), None), P(("row", "col"), None))
    return jax.shard_map(
        on_device, mesh=mesh, in_specs=in_specs, out_specs=out_specs, check_vma=False
    )
```

profile of v0, /device:TPU:0, one launch (start us, length us, event | category | flops | bytes accessed | tf_op | source)
XLA Modules:
  0.0 1146.4 jit_solution(14894379759158796580)
XLA Ops:
  9.2 7.3 all-to-all-start
  16.5 2.1 fusion.3
  18.6 5.0 all-to-all-done
  23.6 2.6 all-to-all-start.1
  27.6 25.2 %all-to-all-done.1 = f32[32,32,256]{2,1,0:T(8,128)S(1)} async-done(((f32[32,32,256]{2,1,0:T(8,128)}), f32[32,32,256]{2,1,0:T(8,128)S(1)}, u32[]{:S(2)}, u32[]{:S(2)}) %all-to-all-start.1) | async-done | bytes 1048608 | tf_op jit(solution)/shard_map/all_to_all | solution.py:53
  52.8 2.0 fusion.1
  54.9 97.8 %reduce.9 = f32[2048,8,512]{2,1,0:T(8,128)} reduce(f32[2048,8,1,512]{3,2,1,0:T(1,128)} %param.6, f32[]{:T(128)} %constant.129), dimensions={2}, to_apply=%param.6.reduce_sub_computation | reduce | bytes 67108864 | tf_op args[0]
  152.7 37.9 %copy.23 = f32[256,8,8,512]{3,1,2,0:T(8,128)} copy(f32[256,8,8,512]{3,2,1,0:T(8,128)} %bitcast.146) | data formatting | bytes 67108864
  190.6 68.4 %convolution_bitcast_fusion.2 = f32[2048,256]{0,1:T(8,128)} fusion(f32[4096,256]{1,0:T(8,128)} %all-gather.4.cloned.1.call-done, f32[2048,4096]{1,0:T(8,128)} %bitcast.143), kind=kOutput, calls=%fused_computation.8 | convolution fusion | flops 25769803776 | bytes 39845888 | tf_op jit(solution)/shard_map/dot_general | solution.py:77
  259.1 1.7 fusion.60
  260.8 32.2 %reduce-scatter.4.cloned.1.call-done = f32[512,256]{0,1:T(8,128)} async-done(((f32[2048,256]{0,1:T(8,128)}), f32[512,256]{0,1:T(8,128)}) %reduce-scatter.4.cloned.1.call-update) | async-done | bytes 524304 | tf_op jit(solution)/shard_map/reduce_scatter | solution.py:83
  293.0 2.4 fusion.59
  295.4 133.0 %all-reduce.10.cloned.1.call-done = (f32[256,256]{0,1:T(8,128)}, f32[256,256]{0,1:T(8,128)}) async-done(((f32[256,256]{0,1:T(8,128)}, f32[256,256]{0,1:T(8,128)}), (f32[256,256]{0,1:T(8,128)}, f32[256,256]{0,1:T(8,128)})) %all-reduce.10.cloned.1.call-update) | async-done | bytes 524304 | tf_op jit(solution)/shard_map/psum | solution.py:32
  431.8 11.7 %cholesky.206 = f32[128,128]{1,0:T(8,128)S(1)} custom-call(f32[128,128]{1,0:T(8,128)S(1)} %cholesky.273), custom_call_target="Cholesky" | custom-call | tf_op jit(solution)/shard_map/jit(cholesky)/cholesky | solution.py:27
  443.6 9.8 custom-call.19
  453.9 11.7 %cholesky.223 = f32[128,128]{1,0:T(8,128)S(1)} custom-call(f32[128,128]{1,0:T(8,128)S(1)} %convolution_subtract_fusion.9), custom_call_target="Cholesky" | custom-call | tf_op jit(solution)/shard_map/jit(cholesky)/cholesky | solution.py:27
  467.1 12.1 %cholesky.172 = f32[128,128]{1,0:T(8,128)S(1)} custom-call(f32[128,128]{1,0:T(8,128)S(1)} %cholesky.270), custom_call_target="Cholesky" | custom-call | tf_op jit(solution)/shard_map/jit(cholesky)/cholesky | solution.py:27
  479.3 9.8 custom-call.17
  489.6 11.7 %cholesky.189 = f32[128,128]{1,0:T(8,128)S(1)} custom-call(f32[128,128]{1,0:T(8,128)S(1)} %convolution_subtract_fusion.10), custom_call_target="Cholesky" | custom-call | tf_op jit(solution)/shard_map/jit(cholesky)/cholesky | solution.py:27
  504.0 4.2 while.6
  506.8 1.4 bitcast_dynamic-update-slice_fusion.6
  508.2 19.7 %custom-call.18 = f32[2,128,128]{1,2,0:T(8,128)S(1)} custom-call(f32[2,128,128]{2,1,0:T(8,128)S(1)} %get-tuple-element.24), custom_call_target="InvertDiagBlocksLowerTriangular" | custom-call | tf_op jit(solution)/shard_map/jit(_cho_solve)/triangular_solve | solution.py:28
  530.8 1.7 fusion.61
  534.0 4.1 while.7
  534.6 1.4 bitcast_dynamic-update-slice_fusion.7
  536.6 1.4 bitcast_dynamic-update-slice_fusion.7
  538.0 19.7 %custom-call.20 = f32[2,128,128]{1,2,0:T(8,128)S(1)} custom-call(f32[2,128,128]{2,1,0:T(8,128)S(1)} %get-tuple-element.25), custom_call_target="InvertDiagBlocksLowerTriangular" | custom-call | tf_op jit(solution)/shard_map/jit(_cho_solve)/triangular_solve | solution.py:28
  557.7 100.8 %all-reduce.6.cloned.1.call-done = f32[256,256]{1,0:T(8,128)} async-done(((f32[256,256]{1,0:T(8,128)}), f32[256,256]{1,0:T(8,128)}) %all-reduce.6.cloned.1.call-update) | async-done | bytes 262160 | tf_op jit(solution)/shard_map/psum | solution.py:32
  663.6 46.0 %all-gather.6.cloned.1.call-done = f32[4096,256]{1,0:T(8,128)} async-done(((f32[512,256]{1,0:T(8,128)}), f32[4096,256]{1,0:T(8,128)}) %all-gather.6.cloned.1.call-update) | async-done | bytes 4194320 | tf_op jit(solution)/shard_map/all_gather | solution.py:79
  709.6 59.2 %convolution_bitcast_fusion.1 = f32[2048,256]{0,1:T(8,128)} fusion(f32[4096,256]{1,0:T(8,128)} %all-gather.6.cloned.1.call-done, f32[2048,4096]{1,0:T(8,128)} %bitcast.144), kind=kOutput, calls=%fused_computation.7 | convolution fusion | flops 25769803776 | bytes 39845888 | tf_op jit(solution)/shard_map/dot_general | solution.py:77
  768.9 34.1 %reduce-scatter.6.cloned.1.call-done = f32[512,256]{0,1:T(8,128)} async-done(((f32[2048,256]{0,1:T(8,128)}), f32[512,256]{0,1:T(8,128)}) %reduce-scatter.6.cloned.1.call-update) | async-done | bytes 524304 | tf_op jit(solution)/shard_map/reduce_scatter | solution.py:83
  802.9 2.4 fusion.62
  806.0 129.7 %all-reduce.8.cloned.1.call-done = f32[256,256]{0,1:T(8,128)} async-done(((f32[256,256]{0,1:T(8,128)}), f32[256,256]{0,1:T(8,128)}) %all-reduce.8.cloned.1.call-update) | async-done | bytes 262160 | tf_op jit(solution)/shard_map/psum | solution.py:92
  938.4 11.7 %cholesky.240 = f32[128,128]{1,0:T(8,128)S(1)} custom-call(f32[128,128]{1,0:T(8,128)S(1)} %cholesky.276), custom_call_target="Cholesky" | custom-call | tf_op jit(solution)/shard_map/jit(cholesky)/cholesky | solution.py:27
  950.2 9.8 custom-call.21
  962.2 11.7 %cholesky.257 = f32[128,128]{1,0:T(8,128)S(1)} custom-call(f32[128,128]{1,0:T(8,128)S(1)} %convolution_subtract_fusion.8), custom_call_target="Cholesky" | custom-call | tf_op jit(solution)/shard_map/jit(cholesky)/cholesky | solution.py:27
  976.6 4.2 while.8
  977.4 1.4 bitcast_dynamic-update-slice_fusion.8
  979.4 1.4 bitcast_dynamic-update-slice_fusion.8
  980.8 19.7 %custom-call.22 = f32[2,128,128]{1,2,0:T(8,128)S(1)} custom-call(f32[2,128,128]{2,1,0:T(8,128)S(1)} %get-tuple-element.26), custom_call_target="InvertDiagBlocksLowerTriangular" | custom-call | tf_op jit(solution)/shard_map/jit(_cho_solve)/triangular_solve | solution.py:28
  1002.8 1.8 fusion.6
  1004.7 46.0 %all-gather.8.cloned.1.call-done = f32[4096,256]{1,0:T(8,128)} async-done(((f32[512,256]{1,0:T(8,128)}), f32[4096,256]{1,0:T(8,128)}) %all-gather.8.cloned.1.call-update) | async-done | bytes 4194320 | tf_op jit(solution)/shard_map/all_gather | solution.py:79
  1050.7 41.6 %convolution_bitcast_fusion = f32[2048,256]{1,0:T(8,128)} fusion(f32[4096,256]{1,0:T(8,128)} %all-gather.8.cloned.1.call-done, f32[2048,4096]{1,0:T(8,128)} %bitcast.145), kind=kOutput, calls=%fused_computation.6 | convolution fusion | flops 25769803776 | bytes 39845888 | tf_op jit(solution)/shard_map/dot_general | solution.py:77
  1092.4 1.8 fusion
  1094.2 29.7 %all_to_all.16 = f32[32,32,256]{2,1,0:T(8,128)S(1)} all-to-all(f32[32,32,256]{2,1,0:T(8,128)S(1)} %bitcast.147), channel_id=1, replica_groups=mesh['row'=8,'col'=4] {'row','col'}, dimensions={0} | all-to-all | bytes 2097152 | tf_op jit(solution)/shard_map/all_to_all | solution.py:105
  1124.0 2.6 fusion.4
  1126.6 11.2 reduce-scatter.8.cloned.1.call-done
  1137.8 1.9 sub.26
  (120 shorter events, 33.1 us)
Async XLA Ops:
  7.2 9.4 copy-start
  9.2 14.5 %all-to-all-start = ((s32[32,1,32]{2,1,0:T(1,128)}), s32[32,1,32]{2,1,0:T(1,128)S(1)}, u32[]{:S(2)}, u32[]{:S(2)}) async-start(s32[32,1,32]{2,1,0:T(1,128)} %sub.23), calls=%async_computation | async-start | bytes 32768 | tf_op jit(solution)/shard_map/all_to_all | solution.py:60
  23.6 29.2 %all-to-all-start.1 = ((f32[32,32,256]{2,1,0:T(8,128)}), f32[32,32,256]{2,1,0:T(8,128)S(1)}, u32[]{:S(2)}, u32[]{:S(2)}) async-start(f32[32,32,256]{2,1,0:T(8,128)} %bitcast), calls=%async_computation.1 | async-start | bytes 2097152 | tf_op jit(solution)/shard_map/all_to_all | solution.py:53
  26.3 164.3 %all-gather.4.cloned.1.call-start = ((), (), s32[]{:S(2)}) async-start(), calls=%async_computation.6 | async-start | bytes 4718592 | tf_op jit(solution)/shard_map/all_gather | solution.py:79
  54.9 238.1 %reduce-scatter.4.cloned.1.call-start = ((), (), s32[]{:S(2)}) async-start(), calls=%async_computation.7 | async-start | bytes 2621440 | tf_op jit(solution)/shard_map/reduce_scatter | solution.py:83
  190.6 68.4 %copy-start.2 = (f32[512,256]{1,0:T(8,128)S(1)}, f32[512,256]{1,0:T(8,128)}, u32[]{:S(2)}) copy-start(f32[512,256]{1,0:T(8,128)} %fusion.1) | copy-start | bytes 1572868
  259.0 169.4 %all-reduce.10.cloned.1.call-start = ((), (), s32[]{:S(2)}) async-start(), calls=%async_computation.14 | async-start | bytes 1048576 | tf_op jit(solution)/shard_map/psum | solution.py:32
  295.4 363.2 %all-reduce.6.cloned.1.call-start = ((), (), s32[]{:S(2)}) async-start(), calls=%async_computation.8 | async-start | bytes 524288 | tf_op jit(solution)/shard_map/psum | solution.py:32
  428.4 99.5 %copy-start.5 = (f32[256,256]{0,1:T(8,128)S(1)}, f32[256,256]{0,1:T(8,128)}, u32[]{:S(2)}) copy-start(f32[256,256]{0,1:T(8,128)} %get-tuple-element.51) | copy-start | bytes 786436
  429.6 100.2 %copy-start.6 = (f32[512,256]{0,1:T(8,128)S(1)}, f32[512,256]{0,1:T(8,128)}, u32[]{:S(2)}) copy-start(f32[512,256]{0,1:T(8,128)} %reduce-scatter.4.cloned.1.call-done) | copy-start | bytes 1572868
  532.5 177.0 %all-gather.6.cloned.1.call-start = ((), (), s32[]{:S(2)}) async-start(), calls=%async_computation.9 | async-start | bytes 4718592 | tf_op jit(solution)/shard_map/all_gather | solution.py:79
  663.5 139.4 %copy-start.3 = (f32[512,256]{1,0:T(8,128)S(1)}, f32[512,256]{1,0:T(8,128)}, u32[]{:S(2)}) copy-start(f32[512,256]{1,0:T(8,128)} %convolution_add_fusion.1) | copy-start | bytes 1572868
  663.5 139.4 %reduce-scatter.6.cloned.1.call-start = ((), (), s32[]{:S(2)}) async-start(), calls=%async_computation.10 | async-start | bytes 2621440 | tf_op jit(solution)/shard_map/reduce_scatter | solution.py:83
  768.8 231.7 %copy-start.8 = (f32[256,256]{1,0:T(8,128)S(1)}, f32[256,256]{1,0:T(8,128)}, u32[]{:S(2)}) copy-start(f32[256,256]{1,0:T(8,128)} %all-reduce.6.cloned.1.call-done) | copy-start | bytes 786436
  768.8 166.9 %all-reduce.8.cloned.1.call-start = ((), (), s32[]{:S(2)}) async-start(), calls=%async_computation.11 | async-start | bytes 524288 | tf_op jit(solution)/shard_map/psum | solution.py:92
  805.3 245.4 %all-gather.8.cloned.1.call-start = ((), (), s32[]{:S(2)}) async-start(), calls=%async_computation.12 | async-start | bytes 4718592 | tf_op jit(solution)/shard_map/all_gather | solution.py:79
  806.0 196.8 %copy-start.7 = (f32[512,256]{0,1:T(8,128)S(1)}, f32[512,256]{0,1:T(8,128)}, u32[]{:S(2)}) copy-start(f32[512,256]{0,1:T(8,128)} %reduce-scatter.6.cloned.1.call-done) | copy-start | bytes 1572868
  937.7 0.7 copy-start.9
  1004.6 87.7 %copy-start.4 = (f32[512,256]{1,0:T(8,128)S(1)}, f32[512,256]{1,0:T(8,128)}, u32[]{:S(2)}) copy-start(f32[512,256]{1,0:T(8,128)} %fusion.6) | copy-start | bytes 1572868
  1004.7 133.1 %reduce-scatter.8.cloned.1.call-start = ((), (), s32[]{:S(2)}) async-start(), calls=%async_computation.13 | async-start | bytes 2621440 | tf_op jit(solution)/shard_map/reduce_scatter | solution.py:83
  1092.3 47.3 %copy-start.1 = (f32[512,256]{1,0:T(8,128)S(1)}, f32[512,256]{1,0:T(8,128)}, u32[]{:S(2)}) copy-start(f32[512,256]{1,0:T(8,128)} %param.7) | copy-start | bytes 1572868
Sparse Core Ops, SparseCore 0:
  55.0 45.4 all-gather.3
  259.1 33.7 reduce-scatter.3
  299.0 129.3 all-reduce.9
  532.7 125.8 all-reduce.5
  663.6 45.9 all-gather.5
  768.9 33.9 reduce-scatter.5
  809.0 126.6 all-reduce.7
  1004.8 45.8 all-gather.7
  1092.5 45.2 reduce-scatter.7
where the time goes:
time: 1160 us; the launch traced here: 1150 us
  waiting for transfers between devices  563 us (49%)
  other arithmetic  267 us (23%)
  matrix products  201 us (17%)
  local copies, waits for them, and re-layouts  55.4 us (5%)
  blocking collectives  29.7 us (3%)
  between operations  18.5 us (2%)
    psum x2, waiting for transfers between devices, residual_gram(): return lax.psum(gram_matrix(residual, residual), ('row', 'col'))  234 us
    dot_general x3, matrix products, apply_operator(): jnp.dot(kkt_tile, lax.all_gather(vector, 'row', axis=0, tiled=True), prec...  169 us
    psum x1, waiting for transfers between devices, on_device(): curvature = lax.psum(gram_matrix(direction, applied), ('row', 'col'))  130 us
    another operation x21, other arithmetic, solve_definite(): factor = jnp.linalg.cholesky(matrix)  104 us
    unnamed x1, other arithmetic  97.8 us
    all_gather x3, waiting for transfers between devices, apply_operator(): lax.all_gather(vector, 'row', axis=0, tiled=True)  92 us
    reduce_scatter x3, waiting for transfers between devices, apply_operator(): lax.psum_scatter(partial_rows, 'col', scatter_dimension=0, tiled=True)  77.4 us
    another operation x7, other arithmetic, solve_definite(): return jax.scipy.linalg.cho_solve((factor, True), right)  59.1 us
  transfers between devices with their start and end apart: 11, of which 10 were waited for; matrix products, arithmetic and copies ran while one was open for 15% of the time, Pallas kernels for 0%

commit v1 on v0

v1 whole, which is shorter than its diff:
```python
import functools

import jax
import jax.numpy as jnp
from jax import lax
from jax.experimental import pallas as pl
from jax.experimental.pallas import tpu as pltpu
from jax.sharding import PartitionSpec as P

RELAXATION = 0.15
AXES = ("row", "col")
LANES = 128
PIVOTS = 32


def gram_matrix(left, right):
    return lax.dot_general(
        left,
        right,
        (((0,), (0,)), ((), ())),
        precision=lax.Precision.HIGHEST,
        preferred_element_type=jnp.float32,
    )


def times_small(left, right):
    return jnp.dot(left, right, precision=lax.Precision.HIGHEST, preferred_element_type=jnp.float32)


def invert_small(matrix):
    side = matrix.shape[0]
    down = lax.broadcasted_iota(jnp.int32, (side, side), 0)
    across = lax.broadcasted_iota(jnp.int32, (side, side), 1)
    for k in range(side):
        scale = 1.0 / matrix[k : k + 1, k : k + 1]
        row = jnp.where(across[:1] == k, scale, matrix[k : k + 1, :] * scale)
        rest = jnp.where(across == k, 0.0, matrix) - matrix[:, k : k + 1] * row
        matrix = jnp.where(down == k, row, rest)
    return matrix


def inverse_kernel(matrix_ref, out_ref):
    side = matrix_ref.shape[0]
    out_ref[...] = matrix_ref[...]
    for start in range(0, side, PIVOTS):
        here = slice(start, start + PIVOTS)
        pivot = invert_small(out_ref[here, here])
        rows = times_small(pivot, out_ref[here, :])
        columns = out_ref[:, here]
        update = times_small(columns, rows)
        corner = times_small(columns, pivot)
        out_ref[...] = out_ref[...] - update
        out_ref[:, here] = -corner
        out_ref[here, :] = rows
        out_ref[here, here] = pivot


def inverse_definite(matrix):
    return pl.pallas_call(
        inverse_kernel,
        out_shape=jax.ShapeDtypeStruct(matrix.shape, jnp.float32),
        name="inverse_definite",
    )(matrix)


def solve_refined(inverse, matrix, right):
    answer = times_small(inverse, right)
    return answer + times_small(inverse, right - times_small(matrix, answer))


def exchange(blocks):
    return lax.all_to_all(blocks, AXES, split_axis=0, concat_axis=0, tiled=True)


def sum_everywhere(stacked, device_count):
    rows, width = stacked.shape
    slab = exchange(stacked.reshape(device_count, rows // device_count, width)).sum(axis=0)
    return exchange(jnp.broadcast_to(slab[None], (device_count,) + slab.shape)).reshape(rows, width)


def split_kernel(where_ref, tile_ref, high_ref, low_ref, *, side):
    block = high_ref.shape[0]
    chunks = high_ref.shape[1] // LANES
    first_row, first_column = where_ref[0], where_ref[1]
    down = lax.broadcasted_iota(jnp.int32, (block, LANES), 0) + pl.program_id(0) * block - first_row
    across = lax.broadcasted_iota(jnp.int32, (block, LANES), 1) - first_column
    gap = jnp.where((down >= 0) & (down < side), across - down, LANES * chunks * 4)
    for chunk in range(chunks):
        piece = tile_ref[pl.ds(chunk, block, stride=chunks), :]
        piece = jnp.where(gap == -chunk * LANES, 0.0, piece)
        high = piece.astype(jnp.bfloat16)
        low = (piece - high.astype(jnp.float32)).astype(jnp.bfloat16)
        high_ref[:, chunk * LANES : (chunk + 1) * LANES] = high
        low_ref[:, chunk * LANES : (chunk + 1) * LANES] = low


def split_matrix(kkt, where, side):
    rows = kkt.shape[0]
    width = kkt.shape[1] * kkt.shape[2] * kkt.shape[3]
    chunks = width // LANES
    block = min(128, rows)
    out = jax.ShapeDtypeStruct((rows, width), jnp.bfloat16)
    return pl.pallas_call(
        functools.partial(split_kernel, side=side),
        grid=(rows // block,),
        in_specs=[
            pl.BlockSpec(memory_space=pltpu.SMEM),
            pl.BlockSpec((block * chunks, LANES), lambda i: (i, 0)),
        ],
        out_specs=[pl.BlockSpec((block, width), lambda i: (i, 0))] * 2,
        out_shape=[out, out],
        name="split_matrix",
    )(where, kkt.reshape(rows * chunks, LANES))


def product_kernel(high_ref, low_ref, vector_ref, out_ref, vector_high, vector_low):
    @pl.when(pl.program_id(0) == 0)
    def _():
        vector = vector_ref[...]
        high = vector.astype(jnp.bfloat16)
        vector_high[...] = high
        vector_low[...] = (vector - high.astype(jnp.float32)).astype(jnp.bfloat16)

    def dot(left, right):
        return jnp.dot(left, right, preferred_element_type=jnp.float32)

    high = high_ref[...]
    small = dot(high, vector_low[...]) + dot(low_ref[...], vector_high[...])
    out_ref[...] = small + dot(high, vector_high[...])


def tile_product(high, low, vector):
    rows, width = high.shape
    count = vector.shape[1]
    block = min(256, rows)
    return pl.pallas_call(
        product_kernel,
        grid=(rows // block,),
        in_specs=[
            pl.BlockSpec((block, width), lambda i: (i, 0)),
            pl.BlockSpec((block, width), lambda i: (i, 0)),
            pl.BlockSpec((width, count), lambda i: (0, 0)),
        ],
        out_specs=pl.BlockSpec((block, count), lambda i: (i, 0)),
        out_shape=jax.ShapeDtypeStruct((rows, count), jnp.float32),
        scratch_shapes=[pltpu.VMEM((width, count), jnp.bfloat16)] * 2,
        name="tile_product",
    )(high, low, vector)


def on_device(kkt, flow_grad, perm):
    highest = lax.Precision.HIGHEST
    device_count = lax.axis_size("row") * lax.axis_size("col")
    block_rows, interval_count = flow_grad.shape
    capacity = 2 * max(1, block_rows // device_count)
    slot_total = device_count * capacity
    owner = perm // block_rows
    local_row = perm % block_rows
    position = jnp.arange(block_rows)
    earlier = (owner[None, :] == owner[:, None]) & (position[None, :] < position[:, None])
    slot_index = jnp.sum(earlier.astype(jnp.int32), axis=1)
    slot_key = owner * capacity + slot_index
    onehot = jnp.arange(slot_total)[:, None] == slot_key[None, :]
    selector = onehot.astype(jnp.float32)
    send_rows = jnp.dot(selector, flow_grad, precision=highest, preferred_element_type=jnp.float32)
    send_index = jnp.sum(jnp.where(onehot, local_row[None, :] + 1, 0), axis=1) - 1
    row_place, col_place = lax.axis_index("row"), lax.axis_index("col")
    where = jnp.stack([col_place, row_place]).astype(jnp.int32) * block_rows
    slab = lax.dynamic_slice(
        kkt, (col_place * block_rows, row_place, 0, 0), (block_rows, 1, 1, block_rows)
    ).reshape(block_rows, block_rows)
    diagonal = jnp.sum(jnp.where(position[:, None] == position[None, :], slab, 0.0), axis=1)[:, None]
    places = jnp.pad(
        send_index.astype(jnp.float32).reshape(device_count, 1, capacity),
        ((0, 0), (0, 0), (0, interval_count - capacity)),
    )
    lane = lax.broadcasted_iota(jnp.int32, places.shape, 2)
    places = jnp.where(lane == capacity, jnp.sum(diagonal), places)
    arrived = exchange(
        jnp.concatenate(
            [send_rows.reshape(device_count, capacity, interval_count), places], axis=1
        )
    )
    received = arrived[:, :capacity]
    received_index = arrived[:, capacity, :capacity].astype(jnp.int32)
    high, low = split_matrix(kkt, where, block_rows)
    shift = jnp.sum(arrived[:, capacity, capacity]) / (device_count * block_rows)
    shifted_diagonal = diagonal - shift
    landing = (position[:, None] == received_index.reshape(slot_total)[None, :]).astype(jnp.float32)
    rhs = jnp.dot(
        landing,
        received.reshape(slot_total, interval_count),
        precision=highest,
        preferred_element_type=jnp.float32,
    )

    def gather(vector):
        return lax.all_gather(vector, "row", axis=0, tiled=True)

    def apply_operator(vector, gathered):
        partial_rows = tile_product(high, low, gathered)
        summed = lax.psum_scatter(partial_rows, "col", scatter_dimension=0, tiled=True)
        return summed + shifted_diagonal * vector

    norm_gram = sum_everywhere(gram_matrix(flow_grad, flow_grad), device_count)

    first = apply_operator(rhs, gather(rhs))
    first, norm_gram = lax.optimization_barrier((first, norm_gram))

    first_gathered = gather(first)
    norm_inverse = inverse_definite(norm_gram)
    sums = sum_everywhere(
        jnp.concatenate([gram_matrix(rhs, first), gram_matrix(first, first)], axis=0), device_count
    )
    first_gathered, sums, norm_inverse = lax.optimization_barrier((first_gathered, sums, norm_inverse))
    second = apply_operator(first, first_gathered)
    cross_gram, image_gram = jnp.split(sums, 2, axis=0)
    identity = jnp.eye(interval_count, dtype=jnp.float32)
    curvature = cross_gram + shift * norm_gram
    step_coef = solve_refined(inverse_definite(curvature), curvature, norm_gram)
    keep = identity - shift * step_coef
    cross = gram_matrix(keep, times_small(cross_gram, step_coef))
    fresh = (
        gram_matrix(keep, times_small(norm_gram, keep))
        - cross
        - cross.T
        + gram_matrix(step_coef, times_small(image_gram, step_coef))
    )
    mixing = keep + solve_refined(norm_inverse, norm_gram, fresh)
    second, mixing, step_coef = lax.optimization_barrier((second, mixing, step_coef))

    second_gathered = gather(second)
    direction = times_small(rhs, mixing) - times_small(first, step_coef)
    applied = shift * direction + times_small(first, mixing) - times_small(second, step_coef)
    curvature = sum_everywhere(gram_matrix(direction, applied), device_count)
    next_coef = solve_refined(inverse_definite(curvature), curvature, fresh)

    moved = times_small(mixing, next_coef)
    both = times_small(step_coef, next_coef)
    on_rhs = step_coef + moved + RELAXATION * (keep - shift * moved)
    on_first = -both - RELAXATION * (step_coef + moved - shift * both)
    on_second = RELAXATION * both
    refined = times_small(rhs, on_rhs) + times_small(first, on_first) + times_small(second, on_second)
    so_far = (
        times_small(rhs, identity - shift * on_rhs)
        - times_small(first, on_rhs + shift * on_first)
        - times_small(second, on_first + shift * on_second)
    )
    back_rows = gram_matrix(landing, refined)
    second_gathered, back_rows = lax.optimization_barrier((second_gathered, back_rows))
    third = apply_operator(second, second_gathered)
    returned = exchange(back_rows.reshape(device_count, capacity, interval_count))
    line_grad = -gram_matrix(selector, returned.reshape(slot_total, interval_count))
    true_residual = so_far - times_small(third, on_second)
    return (line_grad, true_residual)


def solution(mesh):
    in_specs = (P("row", None, "col", None), P(AXES, None), P(AXES))
    out_specs = (P(AXES, None), P(AXES, None))
    return jax.shard_map(
        on_device, mesh=mesh, in_specs=in_specs, out_specs=out_specs, check_vma=False
    )
```

time: 1160 us -> 462 us (0.40)
  waiting for transfers between devices: 563 us -> 56.6 us
  other arithmetic: 267 us -> 8.96 us
  Pallas kernels: 0 us -> 189 us
  matrix products: 201 us -> 36.9 us
  blocking collectives: 29.7 us -> 131 us
  local copies, waits for them, and re-layouts: 55.4 us -> 4.47 us
    psum x3 -> x0, waiting for transfers between devices: 364 us -> none  [the longest x2 234 us: residual_gram(): return lax.psum(gram_matrix(residual, residual), ('row', 'col'))]
    pallas_call x0 -> x7, Pallas kernels: none -> 189 us  [the longest x3 87.5 us: inverse_definite(): pl.pallas_call(inverse_kernel, out_shape=jax.ShapeDtypeStruct(matrix.shap...]
    dot_general x3 -> x0, matrix products: 169 us -> none  [apply_operator(): jnp.dot(kkt_tile, lax.all_gather(vector, 'row', axis=0, tiled=True), prec...]
    another operation x28 -> x0, other arithmetic: 163 us -> none  [the longest x21 104 us: solve_definite(): factor = jnp.linalg.cholesky(matrix)]
    all_to_all x1 -> x5, blocking collectives: 29.7 us -> 131 us  [exchange(): return lax.all_to_all(blocks, AXES, split_axis=0, concat_axis=0, tiled=True)]
    unnamed x1 -> x0, other arithmetic: 97.8 us -> none
    all_gather x3, waiting for transfers between devices: 92 us -> 5.84 us  [gather(): return lax.all_gather(vector, 'row', axis=0, tiled=True)]
    reduce_scatter x3, waiting for transfers between devices: 77.4 us -> 26.7 us  [apply_operator(): lax.psum_scatter(partial_rows, 'col', scatter_dimension=0, tiled=True)]
  transfers between devices with their start and end apart: 11 -> 9, of which waited for: 10 -> 4; matrix products, arithmetic and copies ran while one was open for 15% -> 8% of each run, Pallas kernels for 0% -> 28%
where the time goes in v1:
time: 462 us; the launch traced here: 453 us
  Pallas kernels  189 us (41%)
  blocking collectives  131 us (28%)
  waiting for transfers between devices  56.6 us (12%)
  matrix products  36.9 us (8%)
  between operations  16 us (3%)
  starting transfers between devices  10.3 us (2%)
  other arithmetic  8.96 us (2%)
    all_to_all x5, blocking collectives, exchange(): return lax.all_to_all(blocks, AXES, split_axis=0, concat_axis=0, tiled=True)  131 us
    pallas_call x3, Pallas kernels, inverse_definite(): pl.pallas_call(inverse_kernel, out_shape=jax.ShapeDtypeStruct(matrix.shap...  87.5 us
    pallas_call x3, Pallas kernels, tile_product(): pl.pallas_call(product_kernel, grid=(rows // block,), in_specs=[pl.BlockS...  63.4 us
    pallas_call x1, Pallas kernels, split_matrix(): pl.pallas_call(functools.partial(split_kernel, side=side), grid=(rows //...  38 us
    reduce_scatter x3, waiting for transfers between devices, apply_operator(): lax.psum_scatter(partial_rows, 'col', scatter_dimension=0, tiled=True)  26.7 us
    all_to_all x3, waiting for transfers between devices, exchange(): return lax.all_to_all(blocks, AXES, split_axis=0, concat_axis=0, tiled=True)  24 us
    dot_general x25, matrix products, times_small(): jnp.dot(left, right, precision=lax.Precision.HIGHEST, preferred_element_t...  19.6 us
    dot_general x9, matrix products, gram_matrix(): lax.dot_general(left, right, (((0,), (0,)), ((), ())), precision=lax.Prec...  14.1 us
  transfers between devices with their start and end apart: 9, of which 4 were waited for; matrix products, arithmetic and copies ran while one was open for 8% of the time, Pallas kernels for 28%

profile of v1, /device:TPU:0, one launch (start us, length us, event | category | flops | bytes accessed | tf_op | source)
XLA Modules:
  0.0 453.3 jit_solution(8458955589476674642)
XLA Ops:
  7.2 0.7 add_select_fusion.1
  8.6 2.0 constant_dynamic-slice_fusion
  10.6 0.7 fusion.12
  11.3 1.1 fusion.3
  12.4 0.7 broadcast_select_fusion
  13.2 40.5 %all_to_all.40 = f32[32,33,256]{2,1,0:T(8,128)S(1)} all-to-all(f32[32,33,256]{2,1,0:T(8,128)S(1)} %pad_maximum_fusion), channel_id=1, replica_groups=mesh['row'=8,'col'=4] {'row','col'}, dimensions={0} | all-to-all | bytes 2162688 | tf_op jit(solution)/shard_map/all_to_all | solution.py:72
  54.0 2.0 fusion.1
  56.7 38.0 %split_matrix.1 = (bf16[2048,4096]{1,0:T(8,128)(2,1)}, bf16[2048,4096]{1,0:T(8,128)(2,1)}) custom-call(s32[2]{0:T(128)} %add_multiply_fusion.where_ref, f32[65536,128]{1,0:T(8,128)} %bitcast.81), custom_call_target="tpu_custom_call" | custom-call | tf_op jit(solution)/shard_map/split_matrix/pallas_call | solution.py:103
  94.7 5.8 %all-gather.4.cloned.1.call-done.vector_ref = f32[4096,256]{1,0:T(8,128)} async-done(((f32[512,256]{1,0:T(8,128)}), f32[4096,256]{1,0:T(8,128)}) %all-gather.4.cloned.1.call-update) | async-done | bytes 4194320 | tf_op jit(solution)/shard_map/all_gather | solution.py:198
  100.5 21.1 %tile_product.3 = f32[2048,256]{1,0:T(8,128)} custom-call(bf16[2048,4096]{1,0:T(8,128)(2,1)} %get-tuple-element.14.high_ref, bf16[2048,4096]{1,0:T(8,128)(2,1)} %get-tuple-element.15.low_ref, f32[4096,256]{1,0:T(8,128)} %all-gather.4.cloned.1.call-done.vector_ref), custom_call_target="tpu_custom_call" | custom-call | tf_op jit(solution)/shard_map/tile_product/pallas_call | solution.py:136
  121.7 1.0 convolution_bitcast_fusion.1
  122.7 14.2 %all_to_all.41 = f32[32,8,256]{2,1,0:T(8,128)S(1)} all-to-all(f32[32,8,256]{2,1,0:T(8,128)S(1)} %convolution_bitcast_fusion.1), channel_id=1, replica_groups=mesh['row'=8,'col'=4] {'row','col'}, dimensions={0} | all-to-all | bytes 524288 | tf_op jit(solution)/shard_map/all_to_all | solution.py:72
  137.0 0.7 broadcast_in_dim.30
  137.7 2.6 all-to-all-start.2
  140.5 0.7 slice_reduce_fusion
  141.9 16.4 %reduce-scatter.4.cloned.1.call-done = f32[512,256]{1,0:T(8,128)} async-done(((f32[2048,256]{1,0:T(8,128)}), f32[512,256]{1,0:T(8,128)}) %reduce-scatter.4.cloned.1.call-update) | async-done | bytes 524304 | tf_op jit(solution)/shard_map/reduce_scatter | solution.py:202
  158.2 2.0 multiply_add_fusion.1
  160.2 2.3 fusion.43
  162.6 1.0 fusion.42
  163.7 33.5 %all_to_all.42 = f32[32,16,256]{2,1,0:T(8,128)S(1)} all-to-all(f32[32,16,256]{2,1,0:T(8,128)S(1)} %bitcast.93), channel_id=1, replica_groups=mesh['row'=8,'col'=4] {'row','col'}, dimensions={0} | all-to-all | bytes 1048576 | tf_op jit(solution)/shard_map/all_to_all | solution.py:72
  197.2 0.9 broadcast_in_dim.31
  198.1 3.5 all-to-all-start.4
  201.6 29.2 %inverse_definite.3 = f32[256,256]{1,0:T(8,128)} custom-call(f32[256,256]{1,0:T(8,128)} %bitcast.82), custom_call_target="tpu_custom_call" | custom-call | tf_op jit(solution)/shard_map/inverse_definite/pallas_call | solution.py:59
  230.8 21.1 %tile_product.4 = f32[2048,256]{1,0:T(8,128)} custom-call(bf16[2048,4096]{1,0:T(8,128)(2,1)} %get-tuple-element.14.high_ref, bf16[2048,4096]{1,0:T(8,128)(2,1)} %get-tuple-element.15.low_ref, f32[4096,256]{1,0:T(8,128)} %all-gather.6.cloned.1.call-done.vector_ref), custom_call_target="tpu_custom_call" | custom-call | tf_op jit(solution)/shard_map/tile_product/pallas_call | solution.py:136
  252.9 0.7 multiply_add_fusion.3.matrix_ref
  253.7 29.1 %inverse_definite.4 = f32[256,256]{1,0:T(8,128)} custom-call(f32[256,256]{1,0:T(8,128)} %multiply_add_fusion.3.matrix_ref), custom_call_target="tpu_custom_call" | custom-call | tf_op jit(solution)/shard_map/inverse_definite/pallas_call | solution.py:59
  282.8 1.3 fusion.44
  284.1 1.3 convolution_subtract_fusion.8
  285.5 1.3 convolution_add_fusion.6
  287.2 0.6 fusion.34
  288.8 0.6 fusion.6
  291.4 2.0 multiply_add_fusion
  295.8 1.0 convolution_bitcast_fusion
  296.8 22.2 %all_to_all.43 = f32[32,8,256]{2,1,0:T(8,128)S(1)} all-to-all(f32[32,8,256]{2,1,0:T(8,128)S(1)} %convolution_bitcast_fusion), channel_id=1, replica_groups=mesh['row'=8,'col'=4] {'row','col'}, dimensions={0} | all-to-all | bytes 524288 | tf_op jit(solution)/shard_map/all_to_all | solution.py:72
  319.1 20.6 %all_to_all.44 = f32[32,8,256]{2,1,0:T(8,128)} all-to-all(f32[32,8,256]{2,1,0:T(8,128)S(1)} %broadcast_in_dim.32), channel_id=1, replica_groups=mesh['row'=8,'col'=4] {'row','col'}, dimensions={0} | all-to-all | bytes 524288 | tf_op jit(solution)/shard_map/all_to_all | solution.py:72
  339.8 29.2 %inverse_definite.5 = f32[256,256]{1,0:T(8,128)} custom-call(f32[256,256]{1,0:T(8,128)} %bitcast.92), custom_call_target="tpu_custom_call" | custom-call | tf_op jit(solution)/shard_map/inverse_definite/pallas_call | solution.py:59
  368.9 1.3 fusion.47
  370.2 1.3 convolution_subtract_fusion.5
  371.6 1.3 convolution_add_fusion.3
  375.5 3.1 fusion
  378.6 21.1 %tile_product.5 = f32[2048,256]{1,0:T(8,128)} custom-call(bf16[2048,4096]{1,0:T(8,128)(2,1)} %get-tuple-element.14.high_ref, bf16[2048,4096]{1,0:T(8,128)(2,1)} %get-tuple-element.15.low_ref, f32[4096,256]{1,0:T(8,128)} %all-gather.8.cloned.1.call-done.vector_ref), custom_call_target="tpu_custom_call" | custom-call | tf_op jit(solution)/shard_map/tile_product/pallas_call | solution.py:136
  399.7 3.4 all-to-all-start.7
  403.7 0.6 fusion.16
  405.0 0.6 convolution_subtract_fusion.1
  405.6 24.0 %all-to-all-done.7 = f32[32,32,256]{2,1,0:T(8,128)} async-done(((f32[32,32,256]{2,1,0:T(8,128)}), f32[32,32,256]{2,1,0:T(8,128)}, u32[]{:S(2)}, u32[]{:S(2)}) %all-to-all-start.7) | async-done | bytes 1048608 | tf_op jit(solution)/shard_map/all_to_all | solution.py:72
  429.6 3.9 fusion.4
  433.5 10.3 %reduce-scatter.8.cloned.1.call-done = f32[512,256]{1,0:T(8,128)} async-done(((f32[2048,256]{1,0:T(8,128)}), f32[512,256]{1,0:T(8,128)}) %reduce-scatter.8.cloned.1.call-update) | async-done | bytes 524304 | tf_op jit(solution)/shard_map/reduce_scatter | solution.py:202
  443.8 2.5 convolution_subtract_fusion
  (68 shorter events, 11.9 us)
Async XLA Ops:
  7.2 4.1 copy-start
  7.2 93.3 %all-gather.4.cloned.1.call-start = ((), (), s32[]{:S(2)}) async-start(), calls=%async_computation.11 | async-start | bytes 4718592 | tf_op jit(solution)/shard_map/all_gather | solution.py:198
  56.1 102.2 %reduce-scatter.4.cloned.1.call-start = ((), (), s32[]{:S(2)}) async-start(), calls=%async_computation.12 | async-start | bytes 2621440 | tf_op jit(solution)/shard_map/reduce_scatter | solution.py:202
  121.6 36.6 %copy-start.3 = (f32[512,256]{1,0:T(8,128)S(1)}, f32[512,256]{1,0:T(8,128)}, u32[]{:S(2)}) copy-start(f32[512,256]{1,0:T(8,128)} %fusion.1) | copy-start | bytes 1572868
  137.7 22.5 %all-to-all-start.2 = ((f32[32,8,256]{2,1,0:T(8,128)}), f32[32,8,256]{2,1,0:T(8,128)S(1)}, u32[]{:S(2)}, u32[]{:S(2)}) async-start(f32[32,8,256]{2,1,0:T(8,128)} %broadcast_in_dim.30), calls=%async_computation.3 | async-start | bytes 524288 | tf_op jit(solution)/shard_map/all_to_all | solution.py:72
  140.3 90.5 %all-gather.6.cloned.1.call-start = ((), (), s32[]{:S(2)}) async-start(), calls=%async_computation.13 | async-start | bytes 4718592 | tf_op jit(solution)/shard_map/all_gather | solution.py:198
  160.2 2.4 copy-start.2
  160.2 3.4 copy-start.5
  198.1 32.7 %all-to-all-start.4 = ((f32[32,16,256]{2,1,0:T(8,128)}), f32[32,16,256]{2,1,0:T(8,128)S(1)}, u32[]{:S(2)}, u32[]{:S(2)}) async-start(f32[32,16,256]{2,1,0:T(8,128)} %broadcast_in_dim.31), calls=%async_computation.5 | async-start | bytes 1048576 | tf_op jit(solution)/shard_map/all_to_all | solution.py:72
  201.6 89.8 %reduce-scatter.6.cloned.1.call-start = ((), (), s32[]{:S(2)}) async-start(), calls=%async_computation.14 | async-start | bytes 2621440 | tf_op jit(solution)/shard_map/reduce_scatter | solution.py:202
  252.0 0.9 copy-start.6
  252.0 126.6 %all-gather.8.cloned.1.call-start = ((), (), s32[]{:S(2)}) async-start(), calls=%async_computation.15 | async-start | bytes 4718592 | tf_op jit(solution)/shard_map/all_gather | solution.py:198
  288.0 2.0 copy-start.7
  293.4 150.4 %reduce-scatter.8.cloned.1.call-start = ((), (), s32[]{:S(2)}) async-start(), calls=%async_computation.16 | async-start | bytes 2621440 | tf_op jit(solution)/shard_map/reduce_scatter | solution.py:202
  294.0 1.2 copy-start.4
  399.7 29.9 %all-to-all-start.7 = ((f32[32,32,256]{2,1,0:T(8,128)}), f32[32,32,256]{2,1,0:T(8,128)}, u32[]{:S(2)}, u32[]{:S(2)}) async-start(f32[32,32,256]{2,1,0:T(8,128)} %bitcast.12), calls=%async_computation.9 | async-start | bytes 2097152 | tf_op jit(solution)/shard_map/all_to_all | solution.py:72
  405.0 41.2 %copy-start.1 = (f32[512,256]{1,0:T(8,128)S(1)}, f32[512,256]{1,0:T(8,128)}, u32[]{:S(2)}) copy-start(f32[512,256]{1,0:T(8,128)} %param.4) | copy-start | bytes 1572868
Sparse Core Ops, SparseCore 0:
  56.2 44.2 all-gather.3
  121.8 36.4 reduce-scatter.3
  160.4 69.1 all-gather.5
  252.1 36.5 reduce-scatter.5
  293.5 59.3 all-gather.7
  399.8 43.8 reduce-scatter.7
